TPU v7x, 256 devices: a whole 4x4x8 slice. The times are simulated.
256 devices in a mesh: dp: 8 (over y, core), expert: 32 (over x, z).
Axes of the slice: x: 4, y: 4, z: 8, core: 2. Of those that a mesh axis runs over, the one named last changes fastest.
Arguments:
- hidden_token_tiles: bfloat16 [8, 1024, 1024], P(None, 'dp'), may hold values from -6 to 6
- gradient_token_tiles: bfloat16 [8, 7168, 1024], P(None, 'expert', 'dp'), may hold values from -0.59765625 to 0.59765625
- momentum: float32 [8, 7168, 1024], P('dp', 'expert'), may hold values from -54 to 54, as said below
- filled_tile_count: int32 [8, 8], replicated, may hold values from 1 to 8, as said below
Outputs:
- new_momentum: float32 [8, 7168, 1024], P('dp', 'expert')
- update: float32 [8, 7168, 1024], P(None, 'expert')
Inputs may be any that keep to these rules, and one draw needn't show every extreme that they name: momentum entries are finite reals. filled_tile_count[g, x] filled tiles stand at the head of group g's slots for expert x; in every draw one expert is full in every group.
All inputs are finite; a program needn't handle non-finite values.
Results may differ from a plain program's by a relative error of at most 0.0009.
Values may be sent and summed in bfloat16 or wider, within the bound.
No kernel may reach another device: no remote copies, remote signals or barrier semaphores. Data moves between devices by JAX's collectives and lax.ppermute only.
A program may use at most 64 MiB of HBM per device.

v0:
```python
import math
import jax
import jax.numpy as jnp
from jax import lax
from jax.sharding import PartitionSpec as P

D = 7168
FF = 1024
TILE = 16
ITERS = 2
MOMENTUM_DECAY = 0.95
EPSILON = 1e-07
COEF_A = 3.4445
COEF_B = -4.775
COEF_C = 2.0315


def full_dot(left, right):
    return jnp.dot(left, right, precision=lax.Precision.HIGHEST, preferred_element_type=jnp.float32)


def body(hidden_token_tiles, gradient_token_tiles, momentum, filled_tile_count):
    group = lax.axis_index("dp")
    rows_group = hidden_token_tiles.shape[1]
    experts_here = hidden_token_tiles.shape[0]
    limits = lax.dynamic_index_in_dim(filled_tile_count, group, 0, keepdims=False) * TILE
    positions = lax.broadcasted_iota(jnp.int32, (experts_here, rows_group), 1)
    tallied_tiles = positions < limits[:, None]
    retained_entries = jnp.where(
        tallied_tiles[:, :, None], hidden_token_tiles, jnp.zeros((), jnp.bfloat16)
    )
    gradient = lax.psum_scatter(
        jnp.einsum(
            "tba,tan->tbn",
            gradient_token_tiles,
            retained_entries,
            preferred_element_type=jnp.float32,
        ),
        "dp",
        scatter_dimension=0,
        tiled=True,
    )[0]
    moment = MOMENTUM_DECAY * momentum[0] + gradient
    current = moment
    for iteration in range(ITERS):
        gram_total = lax.psum(full_dot(current.T, current).astype(jnp.bfloat16), "expert").astype(
            jnp.float32
        )
        if iteration == 0:
            factor = 1.0 / (jnp.sqrt(jnp.trace(gram_total)) + EPSILON)
            current = current * factor
            gram_total = gram_total * (factor * factor)
        mixer = COEF_B * gram_total + COEF_C * full_dot(gram_total, gram_total)
        current = COEF_A * current + full_dot(current, mixer)
    update_local = current * math.sqrt(max(FF, D))
    gathered = lax.all_gather(update_local[None], "dp", axis=0, tiled=True)
    return (moment[None], gathered)


def solution(mesh):
    placed = (P(None, "dp", None), P(None, "expert", "dp"), P("dp", "expert", None), P())
    return jax.shard_map(
        body,
        mesh=mesh,
        in_specs=placed,
        out_specs=(P("dp", "expert", None), P(None, "expert", None)),
        check_vma=False,
    )
```

profile of v0, /device:TPU:1, one launch (start us, length us, event | category | flops | bytes accessed | tf_op | source)
XLA Modules:
  0.0 476.9 jit_solution(4458757613890195179)
XLA Ops:
  7.2 0.0 copy-start
  7.2 0.0 reduce-scatter.2.cloned.1.call-start
  7.2 0.7 multiply_bitcast_fusion
  8.0 0.1 iota_compare_fusion.1
  8.0 0.2 copy-done
  8.2 5.8 %convolution_bitcast_fusion = f32[8,224,1024]{2,1,0:T(8,128)} fusion(bf16[8,224,128]{2,1,0:T(8,128)(2,1)S(1)} %copy-done, bf16[8,128,1024]{2,1,0:T(8,128)(2,1)} %param.4, pred[8,128]{1,0:T(8,128)(4,1)S(1)} %iota_compare_fusion.1), kind=kOutput, calls=%fused_computation.14 | convolution fusion | flops 470810624 | bytes 9896960 | tf_op jit(solution)/shard_map/tba,tan->tbn/dot_general | solution.py:33
  14.0 0.0 copy-start.4
  14.0 0.0 reduce-scatter.2.cloned.1.call-update
  14.0 0.0 all-reduce.3.cloned.1.call-start
  14.1 53.4 %reduce-scatter.2.cloned.1.call-done = f32[1,224,1024]{2,1,0:T(8,128)} async-done(((f32[8,224,1024]{2,1,0:T(8,128)}), f32[1,224,1024]{2,1,0:T(8,128)}) %reduce-scatter.2.cloned.1.call-update) | async-done | bytes 917520 | tf_op jit(solution)/shard_map/reduce_scatter | solution.py:32
  67.5 0.0 copy-done.4
  67.5 1.3 multiply_add_fusion
  68.8 0.0 copy-start.2
  68.8 4.8 %convolution_convert_fusion.1 = bf16[1024,1024]{1,0:T(8,128)(2,1)} fusion(f32[1,224,1024]{2,1,0:T(8,128)S(1)} %multiply_add_fusion), kind=kOutput, calls=%fused_computation.24 | convolution fusion | flops 2819620864 | bytes 3014656 | tf_op jit(solution)/shard_map/dot_general | solution.py:19
  73.6 0.0 all-reduce.3.cloned.1.call-update
  73.6 0.2 all-reduce.5.cloned.1.call-start
  73.9 149.9 %all-reduce.3.cloned.1.call-done = bf16[1024,1024]{1,0:T(8,128)(2,1)} async-done(((bf16[1024,1024]{1,0:T(8,128)(2,1)}), bf16[1024,1024]{1,0:T(8,128)(2,1)}) %all-reduce.3.cloned.1.call-update) | async-done | bytes 2097168 | tf_op jit(solution)/shard_map/psum | solution.py:46
  223.7 2.3 fusion.5
  226.8 0.0 copy-start.1
  226.8 16.3 %fusion = f32[1024,1024]{1,0:T(8,128)S(1)} fusion(bf16[1024,1024]{1,0:T(8,128)(2,1)} %all-reduce.3.cloned.1.call-done, f32[]{:T(128)S(6)} %mul.70), kind=kOutput, calls=%fused_computation.2 | convolution fusion | flops 12886999040 | bytes 6291460 | tf_op jit(solution)/shard_map/dot_general | solution.py:19
  243.2 0.0 copy-done.2
  243.2 0.0 copy-done.1
  243.2 4.1 fusion.23
  247.3 4.8 %convolution_convert_fusion = bf16[1024,1024]{1,0:T(8,128)(2,1)} fusion(f32[224,1024]{1,0:T(8,128)S(1)} %fusion.23), kind=kOutput, calls=%fused_computation.23 | convolution fusion | flops 2819620864 | bytes 3014656 | tf_op jit(solution)/shard_map/dot_general | solution.py:19
  252.1 0.0 all-reduce.5.cloned.1.call-update
  252.1 0.0 all-gather.3.cloned.1.call-start
  252.2 151.3 %all-reduce.5.cloned.1.call-done = bf16[1024,1024]{1,0:T(8,128)(2,1)} async-done(((bf16[1024,1024]{1,0:T(8,128)(2,1)}), bf16[1024,1024]{1,0:T(8,128)(2,1)}) %all-reduce.5.cloned.1.call-update) | async-done | bytes 2097168 | tf_op jit(solution)/shard_map/psum | solution.py:46
  403.5 0.0 copy-start.3
  403.5 4.7 fusion.39
  408.2 0.0 copy-done.3
  408.2 4.6 fusion.26
  412.9 0.0 all-gather.3.cloned.1.call-update
  412.9 50.0 %all-gather.3.cloned.1.call-done = f32[1792,1024]{1,0:T(8,128)} async-done(((f32[224,1024]{1,0:T(8,128)}), f32[1792,1024]{1,0:T(8,128)}) %all-gather.3.cloned.1.call-update) | async-done | bytes 7340048 | tf_op jit(solution)/shard_map/all_gather | solution.py:56
  462.9 7.5 %copy.9 = f32[8,224,1024]{2,1,0:T(8,128)} copy(f32[8,224,1024]{2,1,0:T(8,128)} %bitcast.20) | data formatting | bytes 14680064
Async XLA Ops:
  7.2 1.0 copy-start
  7.2 60.3 %reduce-scatter.2.cloned.1.call-start = ((), (), s32[]{:S(2)}) async-start(), calls=%async_computation.1 | async-start | bytes 8257536 | tf_op jit(solution)/shard_map/reduce_scatter | solution.py:32
  14.0 53.4 %copy-start.4 = (f32[1,224,1024]{2,1,0:T(8,128)S(1)}, f32[1,224,1024]{2,1,0:T(8,128)}, u32[]{:S(2)}) copy-start(f32[1,224,1024]{2,1,0:T(8,128)} %param.6) | copy-start | bytes 2752516
  14.0 209.7 %all-reduce.3.cloned.1.call-start = ((), (), s32[]{:S(2)}) async-start(), calls=%async_computation.2 | async-start | bytes 4194304 | tf_op jit(solution)/shard_map/psum | solution.py:46
  68.8 174.4 %copy-start.2 = (f32[1,224,1024]{2,1,0:T(8,128)}, f32[1,224,1024]{2,1,0:T(8,128)S(1)}, u32[]{:S(2)}) copy-start(f32[1,224,1024]{2,1,0:T(8,128)S(1)} %multiply_add_fusion) | copy-start | bytes 2752516
  73.6 329.9 %all-reduce.5.cloned.1.call-start = ((), (), s32[]{:S(2)}) async-start(), calls=%async_computation.3 | async-start | bytes 4194304 | tf_op jit(solution)/shard_map/psum | solution.py:46
  226.8 16.4 %copy-start.1 = (bf16[1024,1024]{1,0:T(8,128)(2,1)S(1)}, bf16[1024,1024]{1,0:T(8,128)(2,1)}, u32[]{:S(2)}) copy-start(bf16[1024,1024]{1,0:T(8,128)(2,1)} %all-reduce.3.cloned.1.call-done) | copy-start | bytes 6291460
  252.1 210.7 %all-gather.3.cloned.1.call-start = ((), (), s32[]{:S(2)}) async-start(), calls=%async_computation.4 | async-start | bytes 8257536 | tf_op jit(solution)/shard_map/all_gather | solution.py:56
  403.5 4.7 copy-start.3
Sparse Core Ops, SparseCore 0:
  14.2 53.2 reduce-scatter.1
  73.7 149.9 all-reduce.2
  252.2 151.2 all-reduce.4
  413.0 49.7 all-gather.2
where the time goes:
time: 477 us
  waiting for transfers between devices  405 us (85%)
  matrix products  45.2 us (9%)
  between operations  14.6 us (3%)
  local copies, waits for them, and re-layouts  7.71 us (2%)
    psum x2, waiting for transfers between devices, body(): lax.psum(full_dot(current.T, current).astype(jnp.bfloat16), 'expert')  301 us
    reduce_scatter x1, waiting for transfers between devices, body(): lax.psum_scatter(jnp.einsum('tba,tan->tbn', gradient_token_tiles, retaine...  53.4 us
    all_gather x1, waiting for transfers between devices, body(): gathered = lax.all_gather(update_local[None], 'dp', axis=0, tiled=True)  50 us
    dot_general x6, matrix products, full_dot(): jnp.dot(left, right, precision=lax.Precision.HIGHEST, preferred_element_t...  39.4 us
  transfers between devices with their start and end apart: 4, of which 4 were waited for; matrix products, arithmetic and copies ran while one was open for 0% of the time, Pallas kernels for 0%

commit v1 on v0

--- a/solution.py
+++ b/solution.py
@@ -53,7 +53,9 @@
         mixer = COEF_B * gram_total + COEF_C * full_dot(gram_total, gram_total)
         current = COEF_A * current + full_dot(current, mixer)
     update_local = current * math.sqrt(max(FF, D))
-    gathered = lax.all_gather(update_local[None], "dp", axis=0, tiled=True)
+    gathered = jnp.concatenate(
+        lax.all_to_all(jnp.stack([update_local[None]] * lax.axis_size("dp")), "dp", 0, 0), axis=0
+    )
     return (moment[None], gathered)
 
 

time: 477 us -> 516 us (1.082)
  blocking collectives: 0 us -> 92.9 us
  waiting for transfers between devices: 405 us -> 355 us
    all_to_all x0 -> x1, blocking collectives: none -> 92.9 us  [body(): lax.all_to_all(jnp.stack([update_local[None]] * lax.axis_size('dp')), 'dp...]
    all_gather x1 -> x0, waiting for transfers between devices: 50 us -> none  [body(): gathered = lax.all_gather(update_local[None], 'dp', axis=0, tiled=True)]
  transfers between devices with their start and end apart: 4 -> 3, of which waited for: 4 -> 3; matrix products, arithmetic and copies ran while one was open for 0% -> 0% of each run, Pallas kernels for 0% -> 0%
where the time goes in v1:
time: 516 us; the launch traced here: 515 us
  waiting for transfers between devices  355 us (69%)
  blocking collectives  92.9 us (18%)
  matrix products  44.3 us (9%)
  between operations  14.6 us (3%)
    psum x2, waiting for transfers between devices, body(): lax.psum(full_dot(current.T, current).astype(jnp.bfloat16), 'expert')  301 us
    all_to_all x1, blocking collectives, body(): lax.all_to_all(jnp.stack([update_local[None]] * lax.axis_size('dp')), 'dp...  92.9 us
    reduce_scatter x1, waiting for transfers between devices, body(): lax.psum_scatter(jnp.einsum('tba,tan->tbn', gradient_token_tiles, retaine...  53.4 us
    dot_general x6, matrix products, full_dot(): jnp.dot(left, right, precision=lax.Precision.HIGHEST, preferred_element_t...  38.5 us
  transfers between devices with their start and end apart: 3, of which 3 were waited for; matrix products, arithmetic and copies ran while one was open for 0% of the time, Pallas kernels for 0%

profile of v1, /device:TPU:1, one launch (start us, length us, event | category | flops | bytes accessed | tf_op | source)
XLA Modules:
  0.0 515.4 jit_solution(15792589795778438290)
XLA Ops:
  7.2 0.0 copy-start
  7.2 0.0 reduce-scatter.2.cloned.1.call-start
  7.2 0.7 multiply_bitcast_fusion
  8.0 0.1 iota_compare_fusion.1
  8.0 0.2 copy-done
  8.2 5.8 %convolution_bitcast_fusion = f32[8,224,1024]{2,1,0:T(8,128)} fusion(bf16[8,224,128]{2,1,0:T(8,128)(2,1)S(1)} %copy-done, bf16[8,128,1024]{2,1,0:T(8,128)(2,1)} %param.4, pred[8,128]{1,0:T(8,128)(4,1)S(1)} %iota_compare_fusion.1), kind=kOutput, calls=%fused_computation.14 | convolution fusion | flops 470810624 | bytes 9896960 | tf_op jit(solution)/shard_map/tba,tan->tbn/dot_general | solution.py:33
  14.0 0.0 copy-start.4
  14.0 0.0 reduce-scatter.2.cloned.1.call-update
  14.0 0.0 all-reduce.3.cloned.1.call-start
  14.1 53.4 %reduce-scatter.2.cloned.1.call-done = f32[1,224,1024]{2,1,0:T(8,128)} async-done(((f32[8,224,1024]{2,1,0:T(8,128)}), f32[1,224,1024]{2,1,0:T(8,128)}) %reduce-scatter.2.cloned.1.call-update) | async-done | bytes 917520 | tf_op jit(solution)/shard_map/reduce_scatter | solution.py:32
  67.5 0.0 copy-done.4
  67.5 1.3 multiply_add_fusion
  68.8 0.0 copy-start.2
  68.8 4.8 convolution_convert_fusion.1
  73.6 0.0 all-reduce.3.cloned.1.call-update
  73.6 0.2 all-reduce.5.cloned.1.call-start
  73.9 149.9 %all-reduce.3.cloned.1.call-done = bf16[1024,1024]{1,0:T(8,128)(2,1)} async-done(((bf16[1024,1024]{1,0:T(8,128)(2,1)}), bf16[1024,1024]{1,0:T(8,128)(2,1)}) %all-reduce.3.cloned.1.call-update) | async-done | bytes 2097168 | tf_op jit(solution)/shard_map/psum | solution.py:46
  223.7 2.3 fusion.5
  226.8 0.0 copy-start.1
  226.8 16.3 %fusion = f32[1024,1024]{1,0:T(8,128)S(1)} fusion(bf16[1024,1024]{1,0:T(8,128)(2,1)} %all-reduce.3.cloned.1.call-done, f32[]{:T(128)S(6)} %mul.70), kind=kOutput, calls=%fused_computation.2 | convolution fusion | flops 12886999040 | bytes 6291460 | tf_op jit(solution)/shard_map/dot_general | solution.py:19
  243.2 0.0 copy-done.2
  243.2 0.0 copy-done.1
  243.2 4.1 fusion.23
  247.3 4.8 convolution_convert_fusion
  252.1 0.0 all-reduce.5.cloned.1.call-update
  252.1 151.4 %all-reduce.5.cloned.1.call-done = bf16[1024,1024]{1,0:T(8,128)(2,1)} async-done(((bf16[1024,1024]{1,0:T(8,128)(2,1)}), bf16[1024,1024]{1,0:T(8,128)(2,1)}) %all-reduce.5.cloned.1.call-update) | async-done | bytes 2097168 | tf_op jit(solution)/shard_map/psum | solution.py:46
  403.5 0.0 copy-start.3
  403.5 4.7 fusion.39
  408.2 0.0 copy-done.3
  408.2 3.7 fusion.26
  411.9 0.9 stack.3
  412.9 92.9 %all_to_all.5 = f32[8,1,224,1024]{3,2,1,0:T(8,128)S(1)} all-to-all(f32[8,1,224,1024]{3,2,1,0:T(8,128)S(1)} %stack.3), channel_id=1, replica_groups=mesh['dp'=8,'expert'=32] {'dp'}, dimensions={0} | all-to-all | bytes 14680064 | tf_op jit(solution)/shard_map/all_to_all | solution.py:57
  505.8 3.0 copy.9
Async XLA Ops:
  7.2 1.0 copy-start
  7.2 60.3 %reduce-scatter.2.cloned.1.call-start = ((), (), s32[]{:S(2)}) async-start(), calls=%async_computation.2 | async-start | bytes 8257536 | tf_op jit(solution)/shard_map/reduce_scatter | solution.py:32
  14.0 53.4 %copy-start.4 = (f32[1,224,1024]{2,1,0:T(8,128)S(1)}, f32[1,224,1024]{2,1,0:T(8,128)}, u32[]{:S(2)}) copy-start(f32[1,224,1024]{2,1,0:T(8,128)} %param.6) | copy-start | bytes 2752516
  14.0 209.7 %all-reduce.3.cloned.1.call-start = ((), (), s32[]{:S(2)}) async-start(), calls=%async_computation.3 | async-start | bytes 4194304 | tf_op jit(solution)/shard_map/psum | solution.py:46
  68.8 174.4 %copy-start.2 = (f32[1,224,1024]{2,1,0:T(8,128)}, f32[1,224,1024]{2,1,0:T(8,128)S(1)}, u32[]{:S(2)}) copy-start(f32[1,224,1024]{2,1,0:T(8,128)S(1)} %multiply_add_fusion) | copy-start | bytes 2752516
  73.6 329.9 %all-reduce.5.cloned.1.call-start = ((), (), s32[]{:S(2)}) async-start(), calls=%async_computation.4 | async-start | bytes 4194304 | tf_op jit(solution)/shard_map/psum | solution.py:46
  226.8 16.4 %copy-start.1 = (bf16[1024,1024]{1,0:T(8,128)(2,1)S(1)}, bf16[1024,1024]{1,0:T(8,128)(2,1)}, u32[]{:S(2)}) copy-start(bf16[1024,1024]{1,0:T(8,128)(2,1)} %all-reduce.3.cloned.1.call-done) | copy-start | bytes 6291460
  403.5 4.7 copy-start.3
Sparse Core Ops, SparseCore 0:
  14.2 53.2 reduce-scatter.1
  73.7 149.9 all-reduce.2
  252.2 151.2 all-reduce.4
